TPU v7x, 32 devices: a whole 2x2x4 slice. The times are simulated.
32 devices in a mesh: fsdp: 16 (over z, y, core), seq: 2 (over x).
Axes of the slice: x: 2, y: 2, z: 4, core: 2. Of those that a mesh axis runs over, the one named last changes fastest.
Arguments:
- tokens: bfloat16 [16, 1024, 1024], P('fsdp', 'seq'), may hold values from -6 to 6
- condition: bfloat16 [16, 1024], P('fsdp'), may hold values from -6 to 6
- w_ada: bfloat16 [1024, 6144], P('fsdp'), may hold values from -0.1875 to 0.1875
- b_ada: bfloat16 [6144], P('fsdp'), may hold values from -3 to 3
- w_qkv: bfloat16 [1024, 3072], P('fsdp'), may hold values from -0.1875 to 0.1875
- b_qv: bfloat16 [2048], P('fsdp'), may hold values from -1.1953125 to 1.1953125
- w_proj: bfloat16 [1024, 1024], P('fsdp'), may hold values from -0.1875 to 0.1875
- b_proj: bfloat16 [1024], P('fsdp'), may hold values from -1.1953125 to 1.1953125
- w_fc1: bfloat16 [1024, 4096], P('fsdp'), may hold values from -0.1875 to 0.1875
- b_fc1: bfloat16 [4096], P('fsdp'), may hold values from -1.1953125 to 1.1953125
- w_fc2: bfloat16 [4096, 1024], P('fsdp'), may hold values from -0.09375 to 0.09375
- b_fc2: bfloat16 [1024], P('fsdp'), may hold values from -1.1953125 to 1.1953125
- cotangent: bfloat16 [16, 1024, 1024], P('fsdp', 'seq'), may hold values from -6 to 6
Outputs:
- out_tokens: bfloat16 [16, 1024, 1024], P('fsdp', 'seq')
- grad_tokens: float32 [16, 1024, 1024], P('fsdp', 'seq')
- grad_condition: float32 [16, 1024], P('fsdp')
- grad_w_ada: float32 [1024, 6144], P('fsdp')
- grad_b_ada: float32 [6144], P('fsdp')
- grad_w_qkv: float32 [1024, 3072], P('fsdp')
- grad_b_qv: float32 [2048], P('fsdp')
- grad_w_proj: float32 [1024, 1024], P('fsdp')
- grad_b_proj: float32 [1024], P('fsdp')
- grad_w_fc1: float32 [1024, 4096], P('fsdp')
- grad_b_fc1: float32 [4096], P('fsdp')
- grad_w_fc2: float32 [4096, 1024], P('fsdp')
- grad_b_fc2: float32 [1024], P('fsdp')
All inputs are finite; a program needn't handle non-finite values.
Results may differ from a plain program's by a relative error of at most 0.018.
The roundings to bfloat16 on the way count: a program that leaves them out, or rounds other values in their place, can miss the bound.
Values may be sent and summed in bfloat16 or wider, within the bound.
A program may use at most 256 MiB of HBM per device.

v0:
```python
from functools import partial
import jax
import jax.numpy as jnp
from jax import lax
from jax.sharding import PartitionSpec as P

HD = 64
norm_eps = 1e-06
block_rows = 512


def layer_norm(values):
    center = values - jnp.mean(values, axis=-1, keepdims=True)
    rscale = lax.rsqrt(jnp.mean(center * center, axis=-1, keepdims=True) + norm_eps)
    return (center * rscale, rscale)


def norm_back(upstream, normed, rscale):
    mean_up = jnp.mean(upstream, axis=-1, keepdims=True)
    mean_cross = jnp.mean(upstream * normed, axis=-1, keepdims=True)
    return rscale * (upstream - mean_up - normed * mean_cross)


def attend_forward(queries, keys_all, values_all):
    seq_len = keys_all.shape[1]
    rows = min(block_rows, seq_len)
    score_scale = queries.shape[-1] ** (-0.5)
    outputs = []
    totals = []
    for offset in range(0, seq_len, rows):
        q_block = queries[:, offset : offset + rows]
        raw_scores = jnp.einsum(
            "bqhd,bkhd->bhqk", q_block, keys_all, preferred_element_type=jnp.float32
        )
        scores = raw_scores * score_scale
        row_max = jnp.max(scores, axis=-1, keepdims=True)
        shifted = jnp.exp(scores - row_max)
        row_total = jnp.sum(shifted, axis=-1, keepdims=True)
        attn_prob = (shifted / row_total).astype(jnp.bfloat16)
        block_out = jnp.einsum(
            "bhqk,bkhd->bqhd", attn_prob, values_all, preferred_element_type=jnp.float32
        )
        outputs.append(block_out.astype(jnp.bfloat16))
        totals.append(row_max + jnp.log(row_total))
    return (jnp.concatenate(outputs, axis=1), jnp.concatenate(totals, axis=2))


def attend_backward(queries, keys_all, values_all, log_total, d_out):
    seq_len = keys_all.shape[1]
    rows = min(block_rows, seq_len)
    score_scale = queries.shape[-1] ** (-0.5)
    grad_keys = jnp.zeros(keys_all.shape, jnp.float32)
    grad_values = jnp.zeros(values_all.shape, jnp.float32)
    grad_queries = []
    for offset in range(0, seq_len, rows):
        q_block = queries[:, offset : offset + rows]
        d_block = d_out[:, offset : offset + rows]
        raw_scores = jnp.einsum(
            "bqhd,bkhd->bhqk", q_block, keys_all, preferred_element_type=jnp.float32
        )
        attn_prob = jnp.exp(raw_scores * score_scale - log_total[:, :, offset : offset + rows])
        grad_values = grad_values + jnp.einsum(
            "bhqk,bqhd->bkhd",
            attn_prob.astype(jnp.bfloat16),
            d_block,
            preferred_element_type=jnp.float32,
        )
        d_prob = jnp.einsum(
            "bqhd,bkhd->bhqk", d_block, values_all, preferred_element_type=jnp.float32
        )
        center = jnp.sum(attn_prob * d_prob, axis=-1, keepdims=True)
        d_raw = (attn_prob * (d_prob - center) * score_scale).astype(jnp.bfloat16)
        grad_queries.append(
            jnp.einsum("bhqk,bkhd->bqhd", d_raw, keys_all, preferred_element_type=jnp.float32)
        )
        grad_keys = grad_keys + jnp.einsum(
            "bhqk,bqhd->bkhd", d_raw, q_block, preferred_element_type=jnp.float32
        )
    grad_q = jnp.concatenate(grad_queries, axis=1).astype(jnp.bfloat16)
    return (grad_q, grad_keys.astype(jnp.bfloat16), grad_values.astype(jnp.bfloat16))


def on_device(
    tokens,
    condition,
    w_ada,
    b_ada,
    w_qkv,
    b_qv,
    w_proj,
    b_proj,
    w_fc1,
    b_fc1,
    w_fc2,
    b_fc2,
    cotangent,
):
    latents, local_len, model_width = tokens.shape
    groups = lax.axis_size("seq")
    head_dim = HD
    group_width = model_width // groups
    per_group = group_width // head_dim
    ada_w, ada_b, qkv_w, qv_b, proj_w, proj_b, fc1_w, fc1_b, fc2_w, fc2_b = (
        lax.all_gather(w_ada, "fsdp", axis=0, tiled=True),
        lax.all_gather(b_ada, "fsdp", axis=0, tiled=True),
        lax.all_gather(w_qkv, "fsdp", axis=0, tiled=True),
        lax.all_gather(b_qv, "fsdp", axis=0, tiled=True),
        lax.all_gather(w_proj, "fsdp", axis=0, tiled=True),
        lax.all_gather(b_proj, "fsdp", axis=0, tiled=True),
        lax.all_gather(w_fc1, "fsdp", axis=0, tiled=True),
        lax.all_gather(b_fc1, "fsdp", axis=0, tiled=True),
        lax.all_gather(w_fc2, "fsdp", axis=0, tiled=True),
        lax.all_gather(b_fc2, "fsdp", axis=0, tiled=True),
    )
    tokens_f = tokens.astype(jnp.float32)
    lifted, silu_back = jax.vjp(jax.nn.silu, condition.astype(jnp.float32))
    lifted_b = lifted.astype(jnp.bfloat16)
    modulation = jnp.dot(lifted_b, ada_w, preferred_element_type=jnp.float32) + ada_b.astype(
        jnp.float32
    )
    shift_one, scale_one, gate_one, shift_two, scale_two, gate_two = jnp.split(
        modulation[:, None, :], 6, axis=-1
    )
    normed_one, rscale_one = layer_norm(tokens_f)
    hidden_one = (normed_one * (1.0 + scale_one) + shift_one).astype(jnp.bfloat16)
    qkv_bias = jnp.concatenate(
        [qv_b[:model_width], jnp.zeros((model_width,), jnp.bfloat16), qv_b[model_width:]]
    ).astype(jnp.float32)
    qkv_tok = (jnp.dot(hidden_one, qkv_w, preferred_element_type=jnp.float32) + qkv_bias).astype(
        jnp.bfloat16
    )
    spread = lax.all_to_all(
        qkv_tok.reshape(latents, local_len, 3, groups, group_width),
        "seq",
        split_axis=3,
        concat_axis=1,
        tiled=True,
    )
    seq_len = spread.shape[1]
    queries = spread[:, :, 0, 0].reshape(latents, seq_len, per_group, head_dim)
    keys_all = spread[:, :, 1, 0].reshape(latents, seq_len, per_group, head_dim)
    values_all = spread[:, :, 2, 0].reshape(latents, seq_len, per_group, head_dim)
    attn_out, log_total = attend_forward(queries, keys_all, values_all)
    returned = lax.all_to_all(
        attn_out.reshape(latents, seq_len, 1, group_width),
        "seq",
        split_axis=1,
        concat_axis=2,
        tiled=True,
    )
    attn_tok = returned.reshape(latents, local_len, model_width)
    branch = jnp.dot(attn_tok, proj_w, preferred_element_type=jnp.float32) + proj_b.astype(
        jnp.float32
    )
    middle = tokens_f + gate_one * branch
    normed_two, rscale_two = layer_norm(middle)
    hidden_two = (normed_two * (1.0 + scale_two) + shift_two).astype(jnp.bfloat16)
    pre_act = jnp.dot(hidden_two, fc1_w, preferred_element_type=jnp.float32) + fc1_b.astype(
        jnp.float32
    )
    act_f, gelu_back = jax.vjp(partial(jax.nn.gelu, approximate=True), pre_act)
    act_b = act_f.astype(jnp.bfloat16)
    mlp_out = jnp.dot(act_b, fc2_w, preferred_element_type=jnp.float32) + fc2_b.astype(jnp.float32)
    result = (middle + gate_two * mlp_out).astype(jnp.bfloat16)
    grad_out = cotangent.astype(jnp.float32)
    d_gate_two = jnp.sum(grad_out * mlp_out, axis=1)
    d_mlp = (grad_out * gate_two).astype(jnp.bfloat16)
    grad_fc2 = jnp.einsum("btf,btd->fd", act_b, d_mlp, preferred_element_type=jnp.float32)
    bias_fc2 = jnp.sum(d_mlp, axis=(0, 1), dtype=jnp.float32)
    d_act = jnp.einsum("btd,fd->btf", d_mlp, fc2_w, preferred_element_type=jnp.float32)
    d_pre = gelu_back(d_act)[0].astype(jnp.bfloat16)
    grad_fc1 = jnp.einsum("btd,btf->df", hidden_two, d_pre, preferred_element_type=jnp.float32)
    bias_fc1 = jnp.sum(d_pre, axis=(0, 1), dtype=jnp.float32)
    d_hidden_two = jnp.einsum("btf,df->btd", d_pre, fc1_w, preferred_element_type=jnp.float32)
    d_shift_two = jnp.sum(d_hidden_two, axis=1)
    d_scale_two = jnp.sum(d_hidden_two * normed_two, axis=1)
    d_middle = grad_out + norm_back(d_hidden_two * (1.0 + scale_two), normed_two, rscale_two)
    d_gate_one = jnp.sum(d_middle * branch, axis=1)
    d_branch = (d_middle * gate_one).astype(jnp.bfloat16)
    grad_proj = jnp.einsum("btk,btd->kd", attn_tok, d_branch, preferred_element_type=jnp.float32)
    bias_proj = jnp.sum(d_branch, axis=(0, 1), dtype=jnp.float32)
    d_attn = jnp.einsum("btd,kd->btk", d_branch, proj_w, preferred_element_type=jnp.float32).astype(
        jnp.bfloat16
    )
    d_heads = lax.all_to_all(
        d_attn.reshape(latents, local_len, groups, group_width),
        "seq",
        split_axis=2,
        concat_axis=1,
        tiled=True,
    )
    d_heads = d_heads.reshape(latents, seq_len, per_group, head_dim)
    grad_q, grad_k, grad_v = attend_backward(queries, keys_all, values_all, log_total, d_heads)
    d_spread = jnp.stack([grad_q, grad_k, grad_v], axis=2).reshape(
        latents, seq_len, 3, 1, group_width
    )
    d_qkv = lax.all_to_all(d_spread, "seq", split_axis=1, concat_axis=3, tiled=True).reshape(
        latents, local_len, 3 * model_width
    )
    grad_qkv = jnp.einsum("btd,bte->de", hidden_one, d_qkv, preferred_element_type=jnp.float32)
    column_sums = jnp.sum(d_qkv, axis=(0, 1), dtype=jnp.float32)
    bias_qv = jnp.concatenate([column_sums[:model_width], column_sums[2 * model_width :]])
    d_hidden_one = jnp.einsum("bte,de->btd", d_qkv, qkv_w, preferred_element_type=jnp.float32)
    d_shift_one = jnp.sum(d_hidden_one, axis=1)
    d_scale_one = jnp.sum(d_hidden_one * normed_one, axis=1)
    grad_input = d_middle + norm_back(d_hidden_one * (1.0 + scale_one), normed_one, rscale_one)
    d_partial = jnp.concatenate(
        [d_shift_one, d_scale_one, d_gate_one, d_shift_two, d_scale_two, d_gate_two], axis=-1
    )
    d_modulation = lax.psum(d_partial, "seq").astype(jnp.bfloat16)
    d_lifted = jnp.einsum("be,ce->bc", d_modulation, ada_w, preferred_element_type=jnp.float32)
    grad_condition = silu_back(d_lifted)[0]
    grad_ada = jnp.einsum("bc,be->ce", lifted_b, d_modulation, preferred_element_type=jnp.float32)
    bias_ada = jnp.sum(d_modulation, axis=0, dtype=jnp.float32)
    total_ada, total_bada = (
        lax.psum_scatter(
            grad_ada.astype(jnp.bfloat16), "fsdp", scatter_dimension=0, tiled=True
        ).astype(jnp.float32),
        lax.psum_scatter(
            bias_ada.astype(jnp.bfloat16), "fsdp", scatter_dimension=0, tiled=True
        ).astype(jnp.float32),
    )
    shard_qkv, shard_bqv, shard_proj, shard_bproj, shard_fc1, shard_bfc1, shard_fc2, shard_bfc2 = (
        lax.psum_scatter(grad_qkv, "fsdp", scatter_dimension=0, tiled=True),
        lax.psum_scatter(bias_qv, "fsdp", scatter_dimension=0, tiled=True),
        lax.psum_scatter(grad_proj, "fsdp", scatter_dimension=0, tiled=True),
        lax.psum_scatter(bias_proj, "fsdp", scatter_dimension=0, tiled=True),
        lax.psum_scatter(grad_fc1, "fsdp", scatter_dimension=0, tiled=True),
        lax.psum_scatter(bias_fc1, "fsdp", scatter_dimension=0, tiled=True),
        lax.psum_scatter(grad_fc2, "fsdp", scatter_dimension=0, tiled=True),
        lax.psum_scatter(bias_fc2, "fsdp", scatter_dimension=0, tiled=True),
    )
    total_qkv, total_bqv, total_proj, total_bproj, total_fc1, total_bfc1, total_fc2, total_bfc2 = (
        lax.psum(
            (
                shard_qkv,
                shard_bqv,
                shard_proj,
                shard_bproj,
                shard_fc1,
                shard_bfc1,
                shard_fc2,
                shard_bfc2,
            ),
            "seq",
        )
    )
    return (
        result,
        grad_input,
        grad_condition,
        total_ada,
        total_bada,
        total_qkv,
        total_bqv,
        total_proj,
        total_bproj,
        total_fc1,
        total_bfc1,
        total_fc2,
        total_bfc2,
    )


def solution(mesh):
    return jax.shard_map(
        on_device,
        mesh=mesh,
        in_specs=(
            P("fsdp", "seq", None),
            P("fsdp", None),
            P("fsdp", None),
            P("fsdp"),
            P("fsdp", None),
            P("fsdp"),
            P("fsdp", None),
            P("fsdp"),
            P("fsdp", None),
            P("fsdp"),
            P("fsdp", None),
            P("fsdp"),
            P("fsdp", "seq", None),
        ),
        out_specs=(
            P("fsdp", "seq", None),
            P("fsdp", "seq", None),
            P("fsdp", None),
            P("fsdp", None),
            P("fsdp"),
            P("fsdp", None),
            P("fsdp"),
            P("fsdp", None),
            P("fsdp"),
            P("fsdp", None),
            P("fsdp"),
            P("fsdp", None),
            P("fsdp"),
        ),
        check_vma=False,
    )
```

profile of v0, /device:TPU:0, one launch (start us, length us, event | category | flops | bytes accessed | tf_op | source)
XLA Modules:
  0.0 1429.1 jit_solution(12914743900525769951)
XLA Ops:
  12.0 23.8 %all-gather.1 = bf16[16,1,128]{2,1,0:T(2,128)(2,1)S(1)} all-gather(bf16[1,1,128]{2,1,0:T(2,128)(2,1)} %bitcast.251), channel_id=1, replica_groups=mesh['fsdp'=16,'seq'=2] {'fsdp'}, dimensions={0}, use_global_device_ids=true | all-gather | bytes 4352 | tf_op jit(solution)/shard_map/all_gather | solution.py:107
  36.5 18.1 %all-gather = bf16[16,1,384]{2,1,0:T(2,128)(2,1)S(1)} all-gather(bf16[1,1,384]{2,1,0:T(2,128)(2,1)S(1)} %reshape.506), channel_id=1, replica_groups=mesh['fsdp'=16,'seq'=2] {'fsdp'}, dimensions={0}, use_global_device_ids=true | all-gather | bytes 13056 | tf_op jit(solution)/shard_map/all_gather | solution.py:105
  56.7 56.9 %all-gather.9.cloned.1.call-done = bf16[1024,6144]{1,0:T(8,128)(2,1)} async-done(((bf16[64,6144]{1,0:T(8,128)(2,1)}), bf16[1024,6144]{1,0:T(8,128)(2,1)}) %all-gather.9.cloned.1.call-update) | async-done | bytes 12582928 | tf_op jit(solution)/shard_map/all_gather | solution.py:104
  113.6 6.3 fusion.96
  120.0 55.6 %all-gather.11.cloned.1.call-done = bf16[1024,3072]{1,0:T(8,128)(2,1)} async-done(((bf16[64,3072]{1,0:T(8,128)(2,1)}), bf16[1024,3072]{1,0:T(8,128)(2,1)}) %all-gather.11.cloned.1.call-update) | async-done | bytes 6291472 | tf_op jit(solution)/shard_map/all_gather | solution.py:106
  175.6 7.8 add_convert_fusion
  183.4 7.1 reshape.484
  191.0 39.7 %all_to_all.63 = bf16[1,512,3,2,512]{4,1,2,0,3:T(8,128)(2,1)S(1)} all-to-all(bf16[1,512,3,2,512]{4,1,2,0,3:T(8,128)(2,1)S(1)} %copy.46), channel_id=1, replica_groups=mesh['fsdp'=16,'seq'=2] {'seq'}, dimensions={3} | all-to-all | bytes 6291456 | tf_op jit(solution)/shard_map/all_to_all | solution.py:132
  237.3 8.6 multiply_reduce_fusion.3
  249.4 5.6 copy-done.1
  262.9 7.8 fusion.72
  275.9 9.0 reduce.38
  287.5 4.5 all-to-all-start.1
  293.8 30.7 %all-reduce.10 = (bf16[1024]{0:T(1024)(128)(2,1)S(1)}, bf16[1024]{0:T(1024)(128)(2,1)S(1)}) all-reduce(bf16[1024]{0:T(1024)(128)(2,1)S(1)} %dynamic-update-slice, bf16[1024]{0:T(1024)(128)(2,1)S(1)} %dynamic-update-slice.1), channel_id=1, replica_groups=mesh['fsdp'=16,'seq'=2] {'fsdp'}, use_global_device_ids=true, to_apply=%add | all-reduce | flops 2048 | bytes 8192
  324.5 17.6 %all-gather.2 = bf16[16,1,256]{2,1,0:T(2,128)(2,1)S(1)} all-gather(bf16[1,1,256]{2,1,0:T(2,128)(2,1)S(1)} %reshape.510), channel_id=1, replica_groups=mesh['fsdp'=16,'seq'=2] {'fsdp'}, dimensions={0}, use_global_device_ids=true | all-gather | bytes 8704 | tf_op jit(solution)/shard_map/all_gather | solution.py:111
  350.3 4.6 fusion.127
  356.6 12.0 fusion.122
  368.6 13.9 convert_reduce_fusion
  382.5 9.8 fusion.55
  393.1 10.4 convert_reduce_fusion.3
  413.4 4.9 fusion.76
  418.4 9.5 all-to-all-done.2
  432.2 8.2 fusion.29
  440.4 8.7 add_convert_fusion.1
  449.1 5.9 copy.58
  455.0 8.1 fusion.90
  463.1 37.1 %fusion.64 = bf16[8,64,512]{2,1,0:T(8,128)(2,1)} fusion(bf16[1024,8,64]{0,2,1:T(8,128)(2,1)S(1)} %bitcast.199, f32[8,512,1024]{2,1,0:T(8,128)} %fusion.90, f32[8,512]{1,0:T(8,128)S(1)} %log_add_fusion, f32[8,512,1024]{2,1,0:T(8,128)} %copy-done), kind=kOutput, calls=%fused_computation.90 | convolution fusion | flops 574886912 | bytes 35143680 | tf_op jit(solution)/shard_map/bhqk,bkhd->bqhd/dot_general | solution.py:74
  503.7 8.1 fusion.89
  511.8 36.6 %fusion.67 = bf16[8,64,512]{2,1,0:T(8,128)(2,1)S(1)} fusion(bf16[1024,8,64]{0,2,1:T(8,128)(2,1)S(1)} %bitcast.200, f32[8,512,1024]{2,1,0:T(8,128)} %fusion.89, f32[8,512]{1,0:T(8,128)S(1)} %log_add_fusion.1, f32[8,512,1024]{2,1,0:T(8,128)} %get-tuple-element.67), kind=kOutput, calls=%fused_computation.91 | convolution fusion | flops 574886912 | bytes 35143680 | tf_op jit(solution)/shard_map/bhqk,bkhd->bqhd/dot_general | solution.py:74
  550.4 30.7 %fusion.11 = f32[8,64,1024]{2,1,0:T(8,128)} fusion(f32[8,512,1024]{2,1,0:T(8,128)} %fusion.89, f32[8,512,1024]{2,1,0:T(8,128)} %get-tuple-element.67, f32[8,512]{1,0:T(8,128)S(1)} %log_add_fusion.1, bf16[1,1024,8,64]{1,3,2,0:T(8,128)(2,1)S(1)} %bitcast.210), kind=kOutput, calls=%fused_computation.21 | convolution fusion | flops 574624768 | bytes 69763072 | tf_op jit(solution)/shard_map/bhqk,bqhd->bkhd/dot_general | solution.py:76
  581.1 31.5 %add_convert_fusion.2 = bf16[8,64,1024]{2,1,0:T(8,128)(2,1)} fusion(f32[8,64,1024]{2,1,0:T(8,128)} %fusion.11, f32[8,512,1024]{2,1,0:T(8,128)} %fusion.90, f32[8,512]{1,0:T(8,128)S(1)} %log_add_fusion, f32[8,512,1024]{2,1,0:T(8,128)} %copy-done, bf16[1,1024,8,64]{1,3,2,0:T(8,128)(2,1)} %bitcast.208), kind=kOutput, calls=%fused_computation.82 | convolution fusion | flops 575673344 | bytes 70811648 | tf_op jit(solution)/shard_map/bhqk,bqhd->bkhd/dot_general | solution.py:76
  612.6 5.9 copy.57
  618.5 8.6 pad_maximum_fusion
  627.1 50.3 %all_to_all.64 = bf16[1,1024,3,1,512]{4,2,3,0,1:T(4,128)(2,1)S(1)} all-to-all(bf16[1,1024,3,1,512]{4,2,3,0,1:T(4,128)(2,1)S(1)} %pad_maximum_fusion), channel_id=1, replica_groups=mesh['fsdp'=16,'seq'=2] {'seq'}, dimensions={1} | all-to-all | bytes 6291456 | tf_op jit(solution)/shard_map/all_to_all | solution.py:197
  681.1 10.5 fusion.117
  691.7 18.5 %fusion.79 = f32[4096,1024]{1,0:T(8,128)} fusion(bf16[1,512,1024]{2,1,0:T(8,128)(2,1)} %param.25, f32[1024]{0:T(1024)S(1)} %bitcast.243, f32[512,4096]{1,0:T(8,128)} %fusion.122, f32[4096]{0:T(1024)S(1)} %bitcast.236), kind=kOutput, calls=%fused_computation.102 | convolution fusion | flops 4317511680 | bytes 26234880 | tf_op jit(solution)/shard_map/btf,btd->fd/dot_general | solution.py:168
  710.8 15.0 %fusion.120 = f32[1024,4096]{1,0:T(8,128)} fusion(bf16[512,4096]{1,0:T(8,128)(2,1)} %copy-done.37, f32[1,512,1024]{2,1,0:T(8,128)} %copy-done.9, f32[1024]{0:T(1024)S(1)} %bitcast.240, f32[1024]{0:T(1024)S(1)} %bitcast.230, f32[512]{0:T(512)S(1)} %add_rsqrt_fusion, f32[512]{0:T(512)S(1)} %broadcast_multiply_fusion.4), kind=kOutput, calls=%fused_computation.165 | convolution fusion | flops 4297588736 | bytes 23080960 | tf_op jit(solution)/shard_map/btd,btf->df/dot_general | solution.py:172
  728.3 61.3 %all-reduce.7 = (f32[2048]{0:T(1024)S(1)}, f32[1024]{0:T(1024)S(1)}, f32[4096]{0:T(1024)S(1)}, f32[1024]{0:T(1024)S(1)}) all-reduce(f32[2048]{0:T(1024)S(1)} %pad_maximum_fusion.2, f32[1024]{0:T(1024)S(1)} %get-tuple-element.47, f32[4096]{0:T(1024)S(1)} %copy-done.21, ...), channel_id=5, replica_groups=mesh['fsdp'=16,'seq'=2] {'fsdp'}, use_global_device_ids=true, to_apply=%region_26.27.clone | all-reduce | flops 8192 | bytes 65536
  789.9 8.1 fusion.51
  800.8 9.9 all-reduce.8
  810.8 7.4 multiply_convert_fusion
  818.3 8.7 reduce-scatter.8.cloned.1.call-done
  827.0 180.7 %reduce-scatter.14.cloned.1.call-done = f32[256,1024]{1,0:T(8,128)} async-done(((f32[4096,1024]{1,0:T(8,128)}), f32[256,1024]{1,0:T(8,128)}) %reduce-scatter.14.cloned.1.call-update) | async-done | bytes 1048592 | tf_op jit(solution)/shard_map/reduce_scatter | solution.py:230
  1007.7 180.6 %reduce-scatter.12.cloned.1.call-done = f32[64,4096]{1,0:T(8,128)} async-done(((f32[1024,4096]{1,0:T(8,128)}), f32[64,4096]{1,0:T(8,128)}) %reduce-scatter.12.cloned.1.call-update) | async-done | bytes 1048592 | tf_op jit(solution)/shard_map/reduce_scatter | solution.py:228
  1188.9 61.3 %all-reduce.2 = bf16[6144]{0:T(1024)(128)(2,1)S(1)} all-reduce(bf16[6144]{0:T(1024)(128)(2,1)S(1)} %convert_reduce_fusion.5), channel_id=3, replica_groups=mesh['fsdp'=16,'seq'=2] {'fsdp'}, use_global_device_ids=true, to_apply=%region_22.23.clone | all-reduce | flops 6144 | bytes 24576
  1250.8 8.7 fusion.95
  1259.5 67.0 %reduce-scatter.6.cloned.1.call-done = bf16[64,6144]{1,0:T(8,128)(2,1)} async-done(((bf16[1024,6144]{1,0:T(8,128)(2,1)}), bf16[64,6144]{1,0:T(8,128)(2,1)}) %reduce-scatter.6.cloned.1.call-update) | async-done | bytes 786448 | tf_op jit(solution)/shard_map/reduce_scatter | solution.py:216
  1328.8 85.2 %all-reduce.13.cloned.1.call-done = (f32[64,3072]{1,0:T(8,128)}, f32[64,1024]{1,0:T(8,128)}, f32[64,4096]{1,0:T(8,128)}, f32[256,1024]{1,0:T(8,128)}) async-done(((f32[64,3072]{1,0:T(8,128)}, f32[64,1024]{1,0:T(8,128)}, f32[64,4096]{1,0:T(8,128)}, f32[256,1024]{1,0:T(8,128)}), (f32[64,3072]{1,0:T(8,128)}, f32[64,1024]{1,0:T(8,128)}, f32[64,4096]{1,0:T(8,128)}, ...) | async-done | bytes 3145744 | tf_op jit(solution)/shard_map/psum | solution.py:234
  (187 shorter events, 84.7 us)
Async XLA Ops:
  7.2 106.4 %all-gather.9.cloned.1.call-start = ((), (), s32[]{:S(2)}) async-start(), calls=%async_computation.9 | async-start | bytes 13369344 | tf_op jit(solution)/shard_map/all_gather | solution.py:104
  7.9 167.6 %all-gather.11.cloned.1.call-start = ((), (), s32[]{:S(2)}) async-start(), calls=%async_computation.10 | async-start | bytes 6684672 | tf_op jit(solution)/shard_map/all_gather | solution.py:106
  8.7 341.7 %all-gather.13.cloned.1.call-start = ((), (), s32[]{:S(2)}) async-start(), calls=%async_computation.11 | async-start | bytes 2228224 | tf_op jit(solution)/shard_map/all_gather | solution.py:108
  9.4 347.2 %all-gather.15.cloned.1.call-start = ((), (), s32[]{:S(2)}) async-start(), calls=%async_computation.12 | async-start | bytes 8912896 | tf_op jit(solution)/shard_map/all_gather | solution.py:110
  10.0 358.7 %all-gather.17.cloned.1.call-start = ((), (), s32[]{:S(2)}) async-start(), calls=%async_computation.13 | async-start | bytes 8912896 | tf_op jit(solution)/shard_map/all_gather | solution.py:112
  54.7 120.8 %copy-start.16 = (f32[512]{0:T(512)}, f32[512]{0:T(512)S(1)}, u32[]{:S(2)}) copy-start(f32[512]{0:T(512)S(1)} %broadcast_multiply_fusion.5) | copy-start | bytes 6148
  56.7 118.9 %copy-start.22 = (f32[512]{0:T(512)}, f32[512]{0:T(512)S(1)}, u32[]{:S(2)}) copy-start(f32[512]{0:T(512)S(1)} %add_rsqrt_fusion.1) | copy-start | bytes 6148
  56.7 118.9 %copy-start.2 = (bf16[1,512,1024]{2,1,0:T(8,128)(2,1)S(1)}, bf16[1,512,1024]{2,1,0:T(8,128)(2,1)}, u32[]{:S(2)}) copy-start(bf16[1,512,1024]{2,1,0:T(8,128)(2,1)} %param.13) | copy-start | bytes 3145732
  119.9 55.6 %copy-start.14 = (f32[1,1,1024]{2,1,0:T(1,128)}, f32[1,1,1024]{2,1,0:T(1,128)S(1)}, u32[]{:S(2)}) copy-start(f32[1,1,1024]{2,1,0:T(1,128)S(1)} %get-tuple-element.56) | copy-start | bytes 12292
  120.0 55.6 %copy-start.26 = (f32[1,1,1024]{2,1,0:T(1,128)}, f32[1,1,1024]{2,1,0:T(1,128)S(1)}, u32[]{:S(2)}) copy-start(f32[1,1,1024]{2,1,0:T(1,128)S(1)} %get-tuple-element.55) | copy-start | bytes 12292
  120.0 236.6 %copy-start.24 = (f32[1,1,1024]{2,1,0:T(1,128)}, f32[1,1,1024]{2,1,0:T(1,128)S(1)}, u32[]{:S(2)}) copy-start(f32[1,1,1024]{2,1,0:T(1,128)S(1)} %get-tuple-element.53) | copy-start | bytes 12292
  233.7 3.6 copy-start.7
  237.3 21.3 %copy-start = (f32[8,512,1024]{2,1,0:T(8,128)}, f32[8,512,1024]{2,1,0:T(8,128)S(1)}, u32[]{:S(2)}) copy-start(f32[8,512,1024]{2,1,0:T(8,128)S(1)} %get-tuple-element.65) | copy-start | bytes 50331652
  245.9 9.1 copy-start.1
  270.8 21.2 %copy-start.33 = (bf16[256]{0:T(256)(128)(2,1)S(1)}, bf16[256]{0:T(256)(128)(2,1)}, u32[]{:S(2)}) copy-start(bf16[256]{0:T(256)(128)(2,1)} %param.22) | copy-start | bytes 1540
  270.8 21.3 %copy-start.29 = (u32[32]{0:T(128)S(1)}, u32[32]{0:T(128)}, u32[]{:S(2)}) copy-start(u32[32]{0:T(128)} %constant.40) | copy-start | bytes 388
  270.8 22.5 %copy-start.34 = (bf16[64]{0:T(256)(128)(2,1)S(1)}, bf16[64]{0:T(256)(128)(2,1)}, u32[]{:S(2)}) copy-start(bf16[64]{0:T(256)(128)(2,1)} %param.24) | copy-start | bytes 388
  270.8 22.8 %copy-start.35 = (bf16[64]{0:T(256)(128)(2,1)S(1)}, bf16[64]{0:T(256)(128)(2,1)}, u32[]{:S(2)}) copy-start(bf16[64]{0:T(256)(128)(2,1)} %param.20) | copy-start | bytes 388
  275.3 75.0 %copy-start.3 = (bf16[1,512,1024]{2,1,0:T(8,128)(2,1)S(1)}, bf16[1,512,1024]{2,1,0:T(8,128)(2,1)}, u32[]{:S(2)}) copy-start(bf16[1,512,1024]{2,1,0:T(8,128)(2,1)} %param.13) | copy-start | bytes 3145732
  287.5 54.6 %all-to-all-start.1 = ((bf16[2,2,131072]{2,1,0:T(2,128)(2,1)}), bf16[2,2,131072]{2,1,0:T(2,128)(2,1)}, u32[]{:S(2)}, u32[]{:S(2)}) async-start(bf16[2,2,131072]{2,1,0:T(2,128)(2,1)} %reshape.533), calls=%async_computation.1 | async-start | bytes 2097152 | tf_op jit(solution)/shard_map/all_to_all | solution.py:144
  324.5 30.5 %copy-start.18 = (f32[1024]{0:T(1024)}, f32[1024]{0:T(1024)S(1)}, u32[]{:S(2)}) copy-start(f32[1024]{0:T(1024)S(1)} %convert_element_type.179) | copy-start | bytes 12292
  356.6 12.0 copy-start.32
  368.6 13.9 copy-start.10
  382.5 9.8 copy-start.37
  382.5 10.6 copy-start.30
  393.1 11.4 copy-start.31
  409.8 18.1 %all-to-all-start.2 = ((bf16[1,512,2,512]{3,1,0,2:T(8,128)(2,1)}), bf16[1,512,2,512]{3,1,0,2:T(8,128)(2,1)S(1)}, u32[]{:S(2)}, u32[]{:S(2)}) async-start(bf16[1,512,2,512]{3,1,0,2:T(8,128)(2,1)} %copy.53), calls=%async_computation.2 | async-start | bytes 2097152 | tf_op jit(solution)/shard_map/all_to_all | solution.py:185
  413.3 404.9 %reduce-scatter.10.cloned.1.call-start = ((), (), s32[]{:S(2)}) async-start(), calls=%async_computation.16 | async-start | bytes 4456448 | tf_op jit(solution)/shard_map/reduce_scatter | solution.py:226
  418.4 408.6 %reduce-scatter.8.cloned.1.call-start = ((), (), s32[]{:S(2)}) async-start(), calls=%async_computation.15 | async-start | bytes 13369344 | tf_op jit(solution)/shard_map/reduce_scatter | solution.py:224
  511.8 38.6 %copy-start.8 = (bf16[1,1024,1,1,512]{1,4,3,2,0:T(8,128)(2,1)S(1)}, bf16[1,1024,1,1,512]{1,4,3,2,0:T(8,128)(2,1)}, u32[]{:S(2)}) copy-start(bf16[1,1024,1,1,512]{1,4,3,2,0:T(8,128)(2,1)} %copy.49) | copy-start | bytes 3145732
  581.1 37.5 %copy-start.5 = (bf16[1,1024,1,1,512]{4,2,3,0,1:T(2,128)(2,1)S(1)}, bf16[1,1024,1,1,512]{4,2,3,0,1:T(2,128)(2,1)}, u32[]{:S(2)}) copy-start(bf16[1,1024,1,1,512]{4,2,3,0,1:T(2,128)(2,1)} %copy.58) | copy-start | bytes 3145732
  581.1 37.5 %copy-start.6 = (bf16[1,512,1,1,512]{4,2,3,0,1:T(2,128)(2,1)S(1)}, bf16[1,512,1,1,512]{4,2,3,0,1:T(2,128)(2,1)}, u32[]{:S(2)}) copy-start(bf16[1,512,1,1,512]{4,2,3,0,1:T(2,128)(2,1)} %copy.56) | copy-start | bytes 1572868
  677.5 3.6 copy-start.15
  677.5 3.6 copy-start.17
  677.5 3.6 copy-start.23
  677.5 3.6 copy-start.27
  691.6 316.1 %reduce-scatter.14.cloned.1.call-start = ((), (), s32[]{:S(2)}) async-start(), calls=%async_computation.18 | async-start | bytes 17825792 | tf_op jit(solution)/shard_map/reduce_scatter | solution.py:230
  710.2 478.1 %reduce-scatter.12.cloned.1.call-start = ((), (), s32[]{:S(2)}) async-start(), calls=%async_computation.17 | async-start | bytes 17825792 | tf_op jit(solution)/shard_map/reduce_scatter | solution.py:228
  725.9 1.9 copy-start.13
  725.9 2.4 copy-start.21
  725.9 600.6 %reduce-scatter.6.cloned.1.call-start = ((), (), s32[]{:S(2)}) async-start(), calls=%async_computation.14 | async-start | bytes 13369344 | tf_op jit(solution)/shard_map/reduce_scatter | solution.py:216
  789.9 8.5 copy-start.4
  789.9 8.5 copy-start.11
  789.9 8.5 copy-start.12
  789.9 8.5 copy-start.19
  798.0 2.7 copy-start.20
  798.0 2.7 copy-start.28
  818.2 595.9 %all-reduce.13.cloned.1.call-start = ((), (), s32[]{:S(2)}) async-start(), calls=%async_computation.19 | async-start | bytes 6291456 | tf_op jit(solution)/shard_map/psum | solution.py:234
  (3 other events, 3.0 us)
Sparse Core Ops, SparseCore 0:
  10.3 103.2 all-gather.8
  115.9 59.6 all-gather.10
  177.7 40.1 all-gather.12
  219.9 73.0 all-gather.14
  295.0 73.1 all-gather.16
  418.5 72.8 reduce-scatter.9
  691.7 135.2 reduce-scatter.7
  831.1 176.5 reduce-scatter.13
  1011.9 176.4 reduce-scatter.11
  1192.2 134.2 reduce-scatter.5
  1328.9 85.0 all-reduce.12
where the time goes:
time: 1440 us; the launch traced here: 1430 us
  waiting for transfers between devices  647 us (45%)
  matrix products  326 us (23%)
  blocking collectives  313 us (22%)
  local copies, waits for them, and re-layouts  73.4 us (5%)
  other arithmetic  42.9 us (3%)
  between operations  17.8 us (1%)
    reduce_scatter x1, waiting for transfers between devices, on_device(): lax.psum_scatter(grad_fc2, 'fsdp', scatter_dimension=0, tiled=True)  181 us
    reduce_scatter x1, waiting for transfers between devices, on_device(): lax.psum_scatter(grad_fc1, 'fsdp', scatter_dimension=0, tiled=True)  181 us
    unnamed x3, blocking collectives  153 us
    psum x1, waiting for transfers between devices, on_device(): lax.psum((shard_qkv, shard_bqv, shard_proj, shard_bproj, shard_fc1, shard...  85.2 us
    dot_general x2, matrix products, attend_backward(): jnp.einsum('bhqk,bkhd->bqhd', d_raw, keys_all, preferred_element_type=jnp...  73.6 us
    reduce_scatter x1, waiting for transfers between devices, on_device(): lax.psum_scatter(grad_ada.astype(jnp.bfloat16), 'fsdp', scatter_dimension...  67 us
    dot_general x2, matrix products, attend_backward(): jnp.einsum('bhqk,bqhd->bkhd', d_raw, q_block, preferred_element_type=jnp....  62.2 us
    all_gather x1, waiting for transfers between devices, on_device(): lax.all_gather(w_ada, 'fsdp', axis=0, tiled=True)  56.9 us
  transfers between devices with their start and end apart: 13, of which 8 were waited for; matrix products, arithmetic and copies ran while one was open for 27% of the time, Pallas kernels for 0%

commit v1 on v0

--- a/solution.py
+++ b/solution.py
@@ -3,6 +3,7 @@
 import jax.numpy as jnp
 from jax import lax
 from jax.sharding import PartitionSpec as P
+from jax.lax import all_to_all, axis_size
 
 HD = 64
 norm_eps = 1e-06
@@ -194,9 +195,13 @@
     d_spread = jnp.stack([grad_q, grad_k, grad_v], axis=2).reshape(
         latents, seq_len, 3, 1, group_width
     )
-    d_qkv = lax.all_to_all(d_spread, "seq", split_axis=1, concat_axis=3, tiled=True).reshape(
-        latents, local_len, 3 * model_width
-    )
+    keep_up_slabs = lambda z: jnp.concatenate(
+        all_to_all(
+            jnp.stack(jnp.split(z, axis_size("seq"), 1)), "seq", split_axis=0, concat_axis=0
+        ),
+        axis=3,
+    )
+    d_qkv = keep_up_slabs(d_spread).reshape(latents, local_len, 3 * model_width)
     grad_qkv = jnp.einsum("btd,bte->de", hidden_one, d_qkv, preferred_element_type=jnp.float32)
     column_sums = jnp.sum(d_qkv, axis=(0, 1), dtype=jnp.float32)
     bias_qv = jnp.concatenate([column_sums[:model_width], column_sums[2 * model_width :]])

time: 1440 us -> 1390 us (0.965)
  local copies, waits for them, and re-layouts: 73.4 us -> 54.9 us
    unnamed x101 -> x99, local copies, waits for them, and re-layouts: 27.8 us -> 29.8 us
  transfers between devices with their start and end apart: 13 -> 13, of which waited for: 8 -> 8; matrix products, arithmetic and copies ran while one was open for 27% -> 25% of each run, Pallas kernels for 0% -> 0%
where the time goes in v1:
time: 1390 us; the launch traced here: 1380 us
  waiting for transfers between devices  646 us (46%)
  matrix products  320 us (23%)
  blocking collectives  302 us (22%)
  local copies, waits for them, and re-layouts  54.9 us (4%)
  other arithmetic  34.5 us (2%)
  between operations  18 us (1%)
    reduce_scatter x1, waiting for transfers between devices, on_device(): lax.psum_scatter(grad_fc2, 'fsdp', scatter_dimension=0, tiled=True)  181 us
    reduce_scatter x1, waiting for transfers between devices, on_device(): lax.psum_scatter(grad_fc1, 'fsdp', scatter_dimension=0, tiled=True)  181 us
    unnamed x3, blocking collectives  154 us
    psum x1, waiting for transfers between devices, on_device(): lax.psum((shard_qkv, shard_bqv, shard_proj, shard_bproj, shard_fc1, shard...  85.2 us
    dot_general x2, matrix products, attend_backward(): jnp.einsum('bhqk,bkhd->bqhd', d_raw, keys_all, preferred_element_type=jnp...  74.1 us
    reduce_scatter x1, waiting for transfers between devices, on_device(): lax.psum_scatter(grad_ada.astype(jnp.bfloat16), 'fsdp', scatter_dimension...  66.4 us
    dot_general x2, matrix products, attend_backward(): jnp.einsum('bhqk,bqhd->bkhd', d_raw, q_block, preferred_element_type=jnp....  60.7 us
    all_gather x1, waiting for transfers between devices, on_device(): lax.all_gather(w_ada, 'fsdp', axis=0, tiled=True)  56.9 us
  transfers between devices with their start and end apart: 13, of which 8 were waited for; matrix products, arithmetic and copies ran while one was open for 25% of the time, Pallas kernels for 0%

profile of v1, /device:TPU:0, one launch (start us, length us, event | category | flops | bytes accessed | tf_op | source)
XLA Modules:
  0.0 1383.5 jit_solution(2176841012532353997)
XLA Ops:
  12.0 23.8 %all-gather.1 = bf16[16,1,128]{2,1,0:T(2,128)(2,1)S(1)} all-gather(bf16[1,1,128]{2,1,0:T(2,128)(2,1)} %bitcast.261), channel_id=1, replica_groups=mesh['fsdp'=16,'seq'=2] {'fsdp'}, dimensions={0}, use_global_device_ids=true | all-gather | bytes 4352 | tf_op jit(solution)/shard_map/all_gather | solution.py:108
  36.5 18.1 %all-gather = bf16[16,1,384]{2,1,0:T(2,128)(2,1)S(1)} all-gather(bf16[1,1,384]{2,1,0:T(2,128)(2,1)S(1)} %reshape.508), channel_id=1, replica_groups=mesh['fsdp'=16,'seq'=2] {'fsdp'}, dimensions={0}, use_global_device_ids=true | all-gather | bytes 13056 | tf_op jit(solution)/shard_map/all_gather | solution.py:106
  56.7 56.9 %all-gather.9.cloned.1.call-done = bf16[1024,6144]{1,0:T(8,128)(2,1)} async-done(((bf16[64,6144]{1,0:T(8,128)(2,1)}), bf16[1024,6144]{1,0:T(8,128)(2,1)}) %all-gather.9.cloned.1.call-update) | async-done | bytes 12582928 | tf_op jit(solution)/shard_map/all_gather | solution.py:105
  113.6 6.3 fusion.96
  120.0 55.6 %all-gather.11.cloned.1.call-done = bf16[1024,3072]{1,0:T(8,128)(2,1)} async-done(((bf16[64,3072]{1,0:T(8,128)(2,1)}), bf16[1024,3072]{1,0:T(8,128)(2,1)}) %all-gather.11.cloned.1.call-update) | async-done | bytes 6291472 | tf_op jit(solution)/shard_map/all_gather | solution.py:107
  175.6 7.8 add_convert_fusion
  183.4 7.1 reshape.485
  191.0 39.6 %all_to_all.53 = bf16[1,512,3,2,512]{4,1,2,0,3:T(8,128)(2,1)S(1)} all-to-all(bf16[1,512,3,2,512]{4,1,2,0,3:T(8,128)(2,1)S(1)} %copy.52), channel_id=1, replica_groups=mesh['fsdp'=16,'seq'=2] {'seq'}, dimensions={3} | all-to-all | bytes 6291456 | tf_op jit(solution)/shard_map/all_to_all | solution.py:133
  233.6 3.6 multiply_reduce_fusion.2
  237.2 8.6 multiply_reduce_fusion.3
  249.3 5.6 copy-done.1
  258.5 4.3 fusion.73
  262.9 7.8 fusion.72
  270.9 4.3 copy.57
  275.7 9.0 reduce.38
  287.3 4.5 all-to-all-start.1
  293.5 30.6 %all-reduce.10 = (bf16[1024]{0:T(1024)(128)(2,1)S(1)}, bf16[1024]{0:T(1024)(128)(2,1)S(1)}) all-reduce(bf16[1024]{0:T(1024)(128)(2,1)S(1)} %dynamic-update-slice, bf16[1024]{0:T(1024)(128)(2,1)S(1)} %dynamic-update-slice.1), channel_id=1, replica_groups=mesh['fsdp'=16,'seq'=2] {'fsdp'}, use_global_device_ids=true, to_apply=%add | all-reduce | flops 2048 | bytes 8192
  324.1 17.7 %all-gather.2 = bf16[16,1,256]{2,1,0:T(2,128)(2,1)S(1)} all-gather(bf16[1,1,256]{2,1,0:T(2,128)(2,1)S(1)} %reshape.512), channel_id=1, replica_groups=mesh['fsdp'=16,'seq'=2] {'fsdp'}, dimensions={0}, use_global_device_ids=true | all-gather | bytes 8704 | tf_op jit(solution)/shard_map/all_gather | solution.py:112
  350.1 4.6 fusion.127
  356.4 12.0 fusion.122
  368.4 13.3 convert_reduce_fusion
  381.7 9.6 fusion.55
  391.7 10.5 convert_reduce_fusion.3
  412.1 4.9 fusion.76
  417.1 9.6 all-to-all-done.2
  431.0 8.4 fusion.90
  439.5 8.5 fusion.89
  447.9 37.1 %fusion.64 = bf16[8,64,512]{2,1,0:T(8,128)(2,1)} fusion(bf16[1024,8,64]{0,2,1:T(8,128)(2,1)S(1)} %bitcast.209, f32[8,512,1024]{2,1,0:T(8,128)} %fusion.90, f32[8,512]{1,0:T(8,128)S(1)} %log_add_fusion, f32[8,512,1024]{2,1,0:T(8,128)} %copy-done), kind=kOutput, calls=%fused_computation.93 | convolution fusion | flops 574886912 | bytes 35143680 | tf_op jit(solution)/shard_map/bhqk,bkhd->bqhd/dot_general | solution.py:75
  485.0 37.1 %fusion.67 = bf16[8,64,512]{2,1,0:T(8,128)(2,1)} fusion(bf16[1024,8,64]{0,2,1:T(8,128)(2,1)S(1)} %bitcast.210, f32[8,512,1024]{2,1,0:T(8,128)} %fusion.89, f32[8,512]{1,0:T(8,128)S(1)} %log_add_fusion.1, f32[8,512,1024]{2,1,0:T(8,128)} %get-tuple-element.69), kind=kOutput, calls=%fused_computation.94 | convolution fusion | flops 574886912 | bytes 35143680 | tf_op jit(solution)/shard_map/bhqk,bkhd->bqhd/dot_general | solution.py:75
  522.1 30.9 %fusion.11 = f32[8,64,1024]{2,1,0:T(8,128)} fusion(f32[8,512,1024]{2,1,0:T(8,128)} %fusion.89, f32[8,512,1024]{2,1,0:T(8,128)} %get-tuple-element.69, f32[8,512]{1,0:T(8,128)S(1)} %log_add_fusion.1, bf16[1,1024,8,64]{1,3,2,0:T(8,128)(2,1)S(1)} %bitcast.219), kind=kOutput, calls=%fused_computation.21 | convolution fusion | flops 574624768 | bytes 69763072 | tf_op jit(solution)/shard_map/bhqk,bqhd->bkhd/dot_general | solution.py:77
  552.9 29.8 %add_convert_fusion.2 = bf16[8,64,1024]{2,1,0:T(8,128)(2,1)S(1)} fusion(f32[8,64,1024]{2,1,0:T(8,128)} %fusion.11, f32[8,512,1024]{2,1,0:T(8,128)} %fusion.90, f32[8,512]{1,0:T(8,128)S(1)} %log_add_fusion, f32[8,512,1024]{2,1,0:T(8,128)} %copy-done, bf16[1,1024,8,64]{1,3,2,0:T(8,128)(2,1)S(1)} %bitcast.220), kind=kOutput, calls=%fused_computation.83 | convolution fusion | flops 575673344 | bytes 70811648 | tf_op jit(solution)/shard_map/bhqk,bqhd->bkhd/dot_general | solution.py:77
  582.8 7.4 fusion.29
  590.2 7.8 add_convert_fusion.1
  599.0 39.0 %all_to_all.54 = bf16[2,1,512,3,1,512]{2,5,3,4,1,0:T(8,128)(2,1)S(1)} all-to-all(bf16[2,1,512,3,1,512]{2,5,3,4,1,0:T(8,128)(2,1)S(1)} %pad_maximum_fusion.1), channel_id=1, replica_groups=mesh['fsdp'=16,'seq'=2] {'seq'}, dimensions={0} | all-to-all | bytes 6291456 | tf_op jit(solution)/shard_map/all_to_all | solution.py:199
  640.1 6.9 fusion.117
  647.2 19.0 %fusion.79 = f32[4096,1024]{1,0:T(8,128)} fusion(bf16[1,512,1024]{2,1,0:T(8,128)(2,1)} %param.25, f32[1024]{0:T(1024)S(1)} %bitcast.253, f32[512,4096]{1,0:T(8,128)} %fusion.122, f32[4096]{0:T(1024)S(1)} %bitcast.246), kind=kOutput, calls=%fused_computation.105 | convolution fusion | flops 4317511680 | bytes 26234880 | tf_op jit(solution)/shard_map/btf,btd->fd/dot_general | solution.py:169
  666.9 14.9 %fusion.120 = f32[1024,4096]{1,0:T(8,128)} fusion(bf16[512,4096]{1,0:T(8,128)(2,1)} %copy-done.36, f32[1,512,1024]{2,1,0:T(8,128)} %copy-done.9, f32[1024]{0:T(1024)S(1)} %bitcast.250, f32[1024]{0:T(1024)S(1)} %bitcast.240, f32[512]{0:T(512)S(1)} %add_rsqrt_fusion, f32[512]{0:T(512)S(1)} %broadcast_multiply_fusion.4), kind=kOutput, calls=%fused_computation.168 | convolution fusion | flops 4297588736 | bytes 23080960 | tf_op jit(solution)/shard_map/btd,btf->df/dot_general | solution.py:173
  684.1 61.6 %all-reduce.7 = (f32[2048]{0:T(1024)S(1)}, f32[1024]{0:T(1024)S(1)}, f32[4096]{0:T(1024)S(1)}, f32[1024]{0:T(1024)S(1)}) all-reduce(f32[2048]{0:T(1024)S(1)} %pad_maximum_fusion.3, f32[1024]{0:T(1024)S(1)} %get-tuple-element.49, f32[4096]{0:T(1024)S(1)} %get-tuple-element.73, ...), channel_id=5, replica_groups=mesh['fsdp'=16,'seq'=2] {'fsdp'}, use_global_device_ids=true, to_apply=%region_26.27.clone | all-reduce | flops 8192 | bytes 65536
  746.0 8.1 fusion.51
  756.8 9.4 all-reduce.8
  766.4 7.4 multiply_convert_fusion
  773.9 7.2 reduce-scatter.8.cloned.1.call-done
  781.1 180.7 %reduce-scatter.14.cloned.1.call-done = f32[256,1024]{1,0:T(8,128)} async-done(((f32[4096,1024]{1,0:T(8,128)}), f32[256,1024]{1,0:T(8,128)}) %reduce-scatter.14.cloned.1.call-update) | async-done | bytes 1048592 | tf_op jit(solution)/shard_map/reduce_scatter | solution.py:235
  961.8 180.6 %reduce-scatter.12.cloned.1.call-done = f32[64,4096]{1,0:T(8,128)} async-done(((f32[1024,4096]{1,0:T(8,128)}), f32[64,4096]{1,0:T(8,128)}) %reduce-scatter.12.cloned.1.call-update) | async-done | bytes 1048592 | tf_op jit(solution)/shard_map/reduce_scatter | solution.py:233
  1142.9 61.8 %all-reduce.2 = bf16[6144]{0:T(1024)(128)(2,1)S(1)} all-reduce(bf16[6144]{0:T(1024)(128)(2,1)S(1)} %convert_reduce_fusion.5), channel_id=3, replica_groups=mesh['fsdp'=16,'seq'=2] {'fsdp'}, use_global_device_ids=true, to_apply=%region_22.23.clone | all-reduce | flops 6144 | bytes 24576
  1205.4 8.6 fusion.95
  1214.0 66.4 %reduce-scatter.6.cloned.1.call-done = bf16[64,6144]{1,0:T(8,128)(2,1)} async-done(((bf16[1024,6144]{1,0:T(8,128)(2,1)}), bf16[64,6144]{1,0:T(8,128)(2,1)}) %reduce-scatter.6.cloned.1.call-update) | async-done | bytes 786448 | tf_op jit(solution)/shard_map/reduce_scatter | solution.py:221
  1282.9 85.2 %all-reduce.13.cloned.1.call-done = (f32[64,3072]{1,0:T(8,128)}, f32[64,1024]{1,0:T(8,128)}, f32[64,4096]{1,0:T(8,128)}, f32[256,1024]{1,0:T(8,128)}) async-done(((f32[64,3072]{1,0:T(8,128)}, f32[64,1024]{1,0:T(8,128)}, f32[64,4096]{1,0:T(8,128)}, f32[256,1024]{1,0:T(8,128)}), (f32[64,3072]{1,0:T(8,128)}, f32[64,1024]{1,0:T(8,128)}, f32[64,4096]{1,0:T(8,128)}, ...) | async-done | bytes 3145744 | tf_op jit(solution)/shard_map/psum | solution.py:239
  (182 shorter events, 65.8 us)
Async XLA Ops:
  7.2 106.4 %all-gather.9.cloned.1.call-start = ((), (), s32[]{:S(2)}) async-start(), calls=%async_computation.9 | async-start | bytes 13369344 | tf_op jit(solution)/shard_map/all_gather | solution.py:105
  7.9 167.6 %all-gather.11.cloned.1.call-start = ((), (), s32[]{:S(2)}) async-start(), calls=%async_computation.10 | async-start | bytes 6684672 | tf_op jit(solution)/shard_map/all_gather | solution.py:107
  8.7 341.4 %all-gather.13.cloned.1.call-start = ((), (), s32[]{:S(2)}) async-start(), calls=%async_computation.11 | async-start | bytes 2228224 | tf_op jit(solution)/shard_map/all_gather | solution.py:109
  9.4 347.0 %all-gather.15.cloned.1.call-start = ((), (), s32[]{:S(2)}) async-start(), calls=%async_computation.12 | async-start | bytes 8912896 | tf_op jit(solution)/shard_map/all_gather | solution.py:111
  10.0 358.4 %all-gather.17.cloned.1.call-start = ((), (), s32[]{:S(2)}) async-start(), calls=%async_computation.13 | async-start | bytes 8912896 | tf_op jit(solution)/shard_map/all_gather | solution.py:113
  54.7 120.8 %copy-start.18 = (f32[512]{0:T(512)}, f32[512]{0:T(512)S(1)}, u32[]{:S(2)}) copy-start(f32[512]{0:T(512)S(1)} %broadcast_multiply_fusion.5) | copy-start | bytes 6148
  56.7 118.9 %copy-start.22 = (f32[512]{0:T(512)}, f32[512]{0:T(512)S(1)}, u32[]{:S(2)}) copy-start(f32[512]{0:T(512)S(1)} %add_rsqrt_fusion.1) | copy-start | bytes 6148
  56.7 118.9 %copy-start.2 = (bf16[1,512,1024]{2,1,0:T(8,128)(2,1)S(1)}, bf16[1,512,1024]{2,1,0:T(8,128)(2,1)}, u32[]{:S(2)}) copy-start(bf16[1,512,1024]{2,1,0:T(8,128)(2,1)} %param.13) | copy-start | bytes 3145732
  119.9 55.6 %copy-start.16 = (f32[1,1,1024]{2,1,0:T(1,128)}, f32[1,1,1024]{2,1,0:T(1,128)S(1)}, u32[]{:S(2)}) copy-start(f32[1,1,1024]{2,1,0:T(1,128)S(1)} %get-tuple-element.58) | copy-start | bytes 12292
  120.0 63.4 %copy-start.26 = (f32[1,1,1024]{2,1,0:T(1,128)}, f32[1,1,1024]{2,1,0:T(1,128)S(1)}, u32[]{:S(2)}) copy-start(f32[1,1,1024]{2,1,0:T(1,128)S(1)} %get-tuple-element.57) | copy-start | bytes 12292
  120.0 236.4 %copy-start.24 = (f32[1,1,1024]{2,1,0:T(1,128)}, f32[1,1,1024]{2,1,0:T(1,128)S(1)}, u32[]{:S(2)}) copy-start(f32[1,1,1024]{2,1,0:T(1,128)S(1)} %get-tuple-element.55) | copy-start | bytes 12292
  233.6 3.6 copy-start.6
  237.2 21.3 %copy-start = (f32[8,512,1024]{2,1,0:T(8,128)}, f32[8,512,1024]{2,1,0:T(8,128)S(1)}, u32[]{:S(2)}) copy-start(f32[8,512,1024]{2,1,0:T(8,128)S(1)} %get-tuple-element.67) | copy-start | bytes 50331652
  245.8 9.1 copy-start.1
  270.7 21.1 %copy-start.32 = (bf16[256]{0:T(256)(128)(2,1)S(1)}, bf16[256]{0:T(256)(128)(2,1)}, u32[]{:S(2)}) copy-start(bf16[256]{0:T(256)(128)(2,1)} %param.22) | copy-start | bytes 1540
  270.7 21.1 %copy-start.28 = (u32[32]{0:T(128)S(1)}, u32[32]{0:T(128)}, u32[]{:S(2)}) copy-start(u32[32]{0:T(128)} %constant.40) | copy-start | bytes 388
  270.7 22.4 %copy-start.33 = (bf16[64]{0:T(256)(128)(2,1)S(1)}, bf16[64]{0:T(256)(128)(2,1)}, u32[]{:S(2)}) copy-start(bf16[64]{0:T(256)(128)(2,1)} %param.24) | copy-start | bytes 388
  270.7 22.6 %copy-start.34 = (bf16[64]{0:T(256)(128)(2,1)S(1)}, bf16[64]{0:T(256)(128)(2,1)}, u32[]{:S(2)}) copy-start(bf16[64]{0:T(256)(128)(2,1)} %param.20) | copy-start | bytes 388
  275.1 75.0 %copy-start.3 = (bf16[1,512,1024]{2,1,0:T(8,128)(2,1)S(1)}, bf16[1,512,1024]{2,1,0:T(8,128)(2,1)}, u32[]{:S(2)}) copy-start(bf16[1,512,1024]{2,1,0:T(8,128)(2,1)} %param.13) | copy-start | bytes 3145732
  287.3 54.6 %all-to-all-start.1 = ((bf16[2,2,131072]{2,1,0:T(2,128)(2,1)}), bf16[2,2,131072]{2,1,0:T(2,128)(2,1)}, u32[]{:S(2)}, u32[]{:S(2)}) async-start(bf16[2,2,131072]{2,1,0:T(2,128)(2,1)} %reshape.535), calls=%async_computation.1 | async-start | bytes 2097152 | tf_op jit(solution)/shard_map/all_to_all | solution.py:145
  324.1 30.6 %copy-start.20 = (f32[1024]{0:T(1024)}, f32[1024]{0:T(1024)S(1)}, u32[]{:S(2)}) copy-start(f32[1024]{0:T(1024)S(1)} %convert_element_type.179) | copy-start | bytes 12292
  354.7 1.3 copy-start.9
  356.4 12.0 copy-start.31
  368.4 13.3 copy-start.10
  381.7 9.7 copy-start.36
  381.7 10.0 copy-start.29
  391.7 11.5 copy-start.30
  408.4 18.3 %all-to-all-start.2 = ((bf16[1,512,2,512]{3,1,0,2:T(8,128)(2,1)}), bf16[1,512,2,512]{3,1,0,2:T(8,128)(2,1)S(1)}, u32[]{:S(2)}, u32[]{:S(2)}) async-start(bf16[1,512,2,512]{3,1,0,2:T(8,128)(2,1)} %copy.59), calls=%async_computation.2 | async-start | bytes 2097152 | tf_op jit(solution)/shard_map/all_to_all | solution.py:186
  412.0 361.9 %reduce-scatter.10.cloned.1.call-start = ((), (), s32[]{:S(2)}) async-start(), calls=%async_computation.16 | async-start | bytes 4456448 | tf_op jit(solution)/shard_map/reduce_scatter | solution.py:231
  417.0 364.0 %reduce-scatter.8.cloned.1.call-start = ((), (), s32[]{:S(2)}) async-start(), calls=%async_computation.15 | async-start | bytes 13369344 | tf_op jit(solution)/shard_map/reduce_scatter | solution.py:229
  485.0 37.1 %copy-start.7 = (bf16[1,1024,1,1,512]{1,4,3,2,0:T(8,128)(2,1)S(1)}, bf16[1,1024,1,1,512]{1,4,3,2,0:T(8,128)(2,1)}, u32[]{:S(2)}) copy-start(bf16[1,1024,1,1,512]{1,4,3,2,0:T(8,128)(2,1)} %copy.55) | copy-start | bytes 3145732
  590.2 7.9 copy-start.13
  590.2 7.9 copy-start.14
  598.6 41.4 %copy-start.4 = (bf16[1,512,1024]{2,1,0:T(8,128)(2,1)S(1)}, bf16[1,512,1024]{2,1,0:T(8,128)(2,1)}, u32[]{:S(2)}) copy-start(bf16[1,512,1024]{2,1,0:T(8,128)(2,1)} %param.13) | copy-start | bytes 3145732
  598.7 41.4 %copy-start.17 = (f32[1,1,1024]{2,1,0:T(1,128)S(1)}, f32[1,1,1024]{2,1,0:T(1,128)}, u32[]{:S(2)}) copy-start(f32[1,1,1024]{2,1,0:T(1,128)} %copy-done.16) | copy-start | bytes 12292
  598.7 41.4 %copy-start.19 = (f32[512]{0:T(512)S(1)}, f32[512]{0:T(512)}, u32[]{:S(2)}) copy-start(f32[512]{0:T(512)} %copy-done.18) | copy-start | bytes 6148
  598.7 41.4 %copy-start.23 = (f32[512]{0:T(512)S(1)}, f32[512]{0:T(512)}, u32[]{:S(2)}) copy-start(f32[512]{0:T(512)} %copy-done.22) | copy-start | bytes 6148
  598.7 41.4 %copy-start.27 = (f32[1,1,1024]{2,1,0:T(1,128)S(1)}, f32[1,1,1024]{2,1,0:T(1,128)}, u32[]{:S(2)}) copy-start(f32[1,1,1024]{2,1,0:T(1,128)} %copy-done.26) | copy-start | bytes 12292
  638.4 1.6 copy-start.8
  647.0 314.8 %reduce-scatter.14.cloned.1.call-start = ((), (), s32[]{:S(2)}) async-start(), calls=%async_computation.18 | async-start | bytes 17825792 | tf_op jit(solution)/shard_map/reduce_scatter | solution.py:235
  666.3 476.1 %reduce-scatter.12.cloned.1.call-start = ((), (), s32[]{:S(2)}) async-start(), calls=%async_computation.17 | async-start | bytes 17825792 | tf_op jit(solution)/shard_map/reduce_scatter | solution.py:233
  681.8 1.8 copy-start.15
  681.8 598.7 %reduce-scatter.6.cloned.1.call-start = ((), (), s32[]{:S(2)}) async-start(), calls=%async_computation.14 | async-start | bytes 13369344 | tf_op jit(solution)/shard_map/reduce_scatter | solution.py:221
  746.0 8.5 copy-start.5
  746.0 8.5 copy-start.11
  746.0 8.5 copy-start.12
  746.0 8.5 copy-start.21
  773.8 594.3 %all-reduce.13.cloned.1.call-start = ((), (), s32[]{:S(2)}) async-start(), calls=%async_computation.19 | async-start | bytes 6291456 | tf_op jit(solution)/shard_map/psum | solution.py:239
  (2 other events, 1.7 us)
Sparse Core Ops, SparseCore 0:
  10.3 103.2 all-gather.8
  115.9 59.6 all-gather.10
  177.7 40.1 all-gather.12
  219.9 73.0 all-gather.14
  295.0 73.2 all-gather.16
  417.2 72.9 reduce-scatter.9
  647.1 133.9 reduce-scatter.7
  785.2 176.5 reduce-scatter.13
  965.9 176.4 reduce-scatter.11
  1146.3 134.1 reduce-scatter.5
  1283.0 85.1 all-reduce.12
